TPU v7x, 256 devices: a whole 4x4x8 slice. The times are simulated.
256 devices in a mesh: clique: 8 (over y_hi, x), copy: 32 (over z, y_lo, core).
Axes of the slice: x: 4, y: 4 (y_hi: 2, y_lo: 2; y = y_hi * 2 + y_lo), z: 8, core: 2. Of those that a mesh axis runs over, the one named last changes fastest.
Arguments:
- out_grad: bfloat16 [524288, 512], P(('clique', 'copy')), may hold values from -6 to 6
- pre_act: bfloat16 [524288, 512], P(('clique', 'copy')), may hold values from -6 to 6
- batch_count: int32 [256], P(('clique', 'copy')), may hold values from 1024 to 2048, as said below
- layer_two: bfloat16 [512, 512], replicated, may hold values from -0.25 to 0.25
- hot_slots: int32 [524288, 10], P(('clique', 'copy')), may hold values from 0 to 4095
- cold_index: int32 [524288, 15], P(('clique', 'copy')), may hold values from 0 to 2047
- hot_feats: bfloat16 [4096, 768], P('clique'), may hold values from -6 to 6
- cold_feats: bfloat16 [524288, 768], P(('clique', 'copy')), may hold values from -6 to 6
Outputs:
- grad_one: float32 [768, 512], replicated
- grad_two: float32 [512, 512], replicated
Inputs may be any that keep to these rules, and one draw needn't show every extreme that they name: `batch_count`: some device has all 2048 rows live in every draw.
All inputs are finite; a program needn't handle non-finite values.
Results may differ from a plain program's by a relative error of at most 0.015.
Values may be sent and summed in bfloat16 or wider, within the bound.
A program may use at most 128 MiB of HBM per device.

v0:
```python
import jax
import jax.numpy as jnp
from jax import lax
from jax.sharding import PartitionSpec as P


def table_sums(index_cols, row_grad, table_rows, fanout):
    block = min(512, table_rows)
    blocks = table_rows // block
    offsets = jnp.arange(block, dtype=jnp.int32)

    def one_block(start):
        wanted = start + offsets
        counts = jnp.zeros((block, index_cols.shape[0]), jnp.float32)
        for column in range(index_cols.shape[1]):
            counts = counts + (index_cols[:, column][None, :] == wanted[:, None]).astype(
                jnp.float32
            )
        summed = jnp.dot(counts.astype(jnp.bfloat16), row_grad, preferred_element_type=jnp.float32)
        return (summed * (1.0 / fanout)).astype(jnp.bfloat16)

    starts = jnp.arange(blocks, dtype=jnp.int32) * block
    parts = lax.map(one_block, starts)
    return parts.reshape(table_rows, row_grad.shape[1])


def on_device(
    out_grad, pre_act, batch_count, layer_two, hot_slots, cold_index, hot_feats, cold_feats
):
    rows = out_grad.shape[0]
    hot_local = hot_feats.shape[0]
    hot_total = hot_local * lax.axis_size("clique")
    k_hot = hot_slots.shape[1]
    k_cold = cold_index.shape[1]
    fanout = k_hot + k_cold
    cold_rows = cold_feats.shape[0]
    live = (jnp.arange(rows, dtype=jnp.int32) < batch_count[0])[:, None]
    masked = jnp.where(live, out_grad, jnp.zeros_like(out_grad))
    activ = jnp.maximum(pre_act, jnp.zeros_like(pre_act))
    grad_two = jnp.dot(activ.T, masked, preferred_element_type=jnp.float32)
    back = jnp.dot(masked, layer_two.T, preferred_element_type=jnp.float32)
    row_grad = jnp.where(pre_act > 0, back, jnp.zeros_like(back)).astype(jnp.bfloat16)
    hot_part = table_sums(hot_slots, row_grad, hot_total, fanout)
    summed = lax.psum(hot_part, "clique").astype(jnp.float32)
    owned = lax.dynamic_slice_in_dim(summed, lax.axis_index("clique") * hot_local, hot_local, 0)
    cold_part = table_sums(cold_index, row_grad, cold_rows, fanout)
    grad_one = jnp.dot(cold_feats.T, cold_part, preferred_element_type=jnp.float32)
    grad_one = grad_one + jnp.dot(
        hot_feats.T, owned.astype(jnp.bfloat16), preferred_element_type=jnp.float32
    )
    total_one, total_two = lax.psum((grad_one, grad_two), ("clique", "copy"))
    return (total_one, total_two)


def solution(mesh):
    placed = (
        P(("clique", "copy"), None),
        P(("clique", "copy"), None),
        P(("clique", "copy")),
        P(),
        P(("clique", "copy"), None),
        P(("clique", "copy"), None),
        P("clique", None),
        P(("clique", "copy"), None),
    )
    return jax.shard_map(
        on_device, mesh=mesh, in_specs=placed, out_specs=(P(), P()), check_vma=False
    )
```

profile of v0, /device:TPU:2, one launch (start us, length us, event | category | flops | bytes accessed | tf_op | source)
XLA Modules:
  0.0 475.0 jit_solution(12058573302038147682)
XLA Ops:
  8.1 5.2 %select_convert_fusion = bf16[2048,512]{1,0:T(8,128)(2,1)} fusion(bf16[2048,512]{1,0:T(8,128)(2,1)} %param.13, bf16[512,512]{1,0:T(8,128)(2,1)} %param.15, bf16[2048,512]{1,0:T(8,128)(2,1)} %param.12, pred[2048]{0:T(1024)(128)(4,1)S(1)} %iota_compare_fusion), kind=kOutput, calls=%fused_computation.43 | convolution fusion | flops 1077936128 | bytes 6817792 | tf_op jit(solution)/shard_map/dot_general | solution.py:41
  13.2 63.4 %while.23 = (s32[]{:T(128)}, bf16[8,512,512]{2,1,0:T(8,128)(2,1)}, s32[2048,10]{0,1:T(8,128)S(1)}, s32[8]{0:T(128)S(1)}, bf16[2048,512]{1,0:T(8,128)(2,1)}, /*index=5*/s32[]{:T(128)}) while((s32[]{:T(128)}, bf16[8,512,512]{2,1,0:T(8,128)(2,1)}, s32[2048,10]{0,1:T(8,128)S(1)}, s32[8]{0:T(128)S(1)}, bf16[2048,512]{1,0:T(8,128)(2,1)}, ...), condition=%wide.region_3.4_spmd.clone, body=%wide.region_2.3_spmd.clone.sunk | while | flops 1105723904 | bytes 2871893 | solution.py:23
  13.3 0.6 dynamic_slice.22
  13.9 0.6 iota_add_fusion.5
  14.6 6.6 %fusion.68 = bf16[8,512,512]{2,1,0:T(8,128)(2,1)} fusion(bf16[8,512,512]{2,1,0:T(8,128)(2,1)} %get-tuple-element.278, s32[]{:T(128)} %get-tuple-element.277, bf16[2048,512]{1,0:T(8,128)(2,1)} %get-tuple-element.287, s32[2048]{0:T(1024)S(1)} %bitcast.126, s32[2048]{0:T(1024)S(1)} %bitcast.127, s32[2048]{0:T(1024)S(1)} %bitcast.128, ...), kind=kOutput, calls=%fused_computation.41.clone.1 | convolution fusion | flops 1105723392 | bytes 2705920 | tf_op jit(solution)/shard_map/while/body/eval_jaxpr/dot_general | solution.py:19
  21.2 0.6 dynamic_slice.22
  21.9 0.6 iota_add_fusion.5
  22.5 6.6 %fusion.68 = bf16[8,512,512]{2,1,0:T(8,128)(2,1)} fusion(bf16[8,512,512]{2,1,0:T(8,128)(2,1)} %get-tuple-element.278, s32[]{:T(128)} %get-tuple-element.277, bf16[2048,512]{1,0:T(8,128)(2,1)} %get-tuple-element.287, s32[2048]{0:T(1024)S(1)} %bitcast.126, s32[2048]{0:T(1024)S(1)} %bitcast.127, s32[2048]{0:T(1024)S(1)} %bitcast.128, ...), kind=kOutput, calls=%fused_computation.41.clone.1 | convolution fusion | flops 1105723392 | bytes 2705920 | tf_op jit(solution)/shard_map/while/body/eval_jaxpr/dot_general | solution.py:19
  29.2 0.6 dynamic_slice.22
  29.8 0.6 iota_add_fusion.5
  30.4 6.6 %fusion.68 = bf16[8,512,512]{2,1,0:T(8,128)(2,1)} fusion(bf16[8,512,512]{2,1,0:T(8,128)(2,1)} %get-tuple-element.278, s32[]{:T(128)} %get-tuple-element.277, bf16[2048,512]{1,0:T(8,128)(2,1)} %get-tuple-element.287, s32[2048]{0:T(1024)S(1)} %bitcast.126, s32[2048]{0:T(1024)S(1)} %bitcast.127, s32[2048]{0:T(1024)S(1)} %bitcast.128, ...), kind=kOutput, calls=%fused_computation.41.clone.1 | convolution fusion | flops 1105723392 | bytes 2705920 | tf_op jit(solution)/shard_map/while/body/eval_jaxpr/dot_general | solution.py:19
  37.1 0.6 dynamic_slice.22
  37.7 0.6 iota_add_fusion.5
  38.4 6.6 %fusion.68 = bf16[8,512,512]{2,1,0:T(8,128)(2,1)} fusion(bf16[8,512,512]{2,1,0:T(8,128)(2,1)} %get-tuple-element.278, s32[]{:T(128)} %get-tuple-element.277, bf16[2048,512]{1,0:T(8,128)(2,1)} %get-tuple-element.287, s32[2048]{0:T(1024)S(1)} %bitcast.126, s32[2048]{0:T(1024)S(1)} %bitcast.127, s32[2048]{0:T(1024)S(1)} %bitcast.128, ...), kind=kOutput, calls=%fused_computation.41.clone.1 | convolution fusion | flops 1105723392 | bytes 2705920 | tf_op jit(solution)/shard_map/while/body/eval_jaxpr/dot_general | solution.py:19
  45.0 0.6 dynamic_slice.22
  45.6 0.6 iota_add_fusion.5
  46.3 6.6 %fusion.68 = bf16[8,512,512]{2,1,0:T(8,128)(2,1)} fusion(bf16[8,512,512]{2,1,0:T(8,128)(2,1)} %get-tuple-element.278, s32[]{:T(128)} %get-tuple-element.277, bf16[2048,512]{1,0:T(8,128)(2,1)} %get-tuple-element.287, s32[2048]{0:T(1024)S(1)} %bitcast.126, s32[2048]{0:T(1024)S(1)} %bitcast.127, s32[2048]{0:T(1024)S(1)} %bitcast.128, ...), kind=kOutput, calls=%fused_computation.41.clone.1 | convolution fusion | flops 1105723392 | bytes 2705920 | tf_op jit(solution)/shard_map/while/body/eval_jaxpr/dot_general | solution.py:19
  52.9 0.6 dynamic_slice.22
  53.6 0.6 iota_add_fusion.5
  54.2 6.6 %fusion.68 = bf16[8,512,512]{2,1,0:T(8,128)(2,1)} fusion(bf16[8,512,512]{2,1,0:T(8,128)(2,1)} %get-tuple-element.278, s32[]{:T(128)} %get-tuple-element.277, bf16[2048,512]{1,0:T(8,128)(2,1)} %get-tuple-element.287, s32[2048]{0:T(1024)S(1)} %bitcast.126, s32[2048]{0:T(1024)S(1)} %bitcast.127, s32[2048]{0:T(1024)S(1)} %bitcast.128, ...), kind=kOutput, calls=%fused_computation.41.clone.1 | convolution fusion | flops 1105723392 | bytes 2705920 | tf_op jit(solution)/shard_map/while/body/eval_jaxpr/dot_general | solution.py:19
  60.9 0.6 dynamic_slice.22
  61.5 0.6 iota_add_fusion.5
  62.1 6.6 %fusion.68 = bf16[8,512,512]{2,1,0:T(8,128)(2,1)} fusion(bf16[8,512,512]{2,1,0:T(8,128)(2,1)} %get-tuple-element.278, s32[]{:T(128)} %get-tuple-element.277, bf16[2048,512]{1,0:T(8,128)(2,1)} %get-tuple-element.287, s32[2048]{0:T(1024)S(1)} %bitcast.126, s32[2048]{0:T(1024)S(1)} %bitcast.127, s32[2048]{0:T(1024)S(1)} %bitcast.128, ...), kind=kOutput, calls=%fused_computation.41.clone.1 | convolution fusion | flops 1105723392 | bytes 2705920 | tf_op jit(solution)/shard_map/while/body/eval_jaxpr/dot_general | solution.py:19
  68.8 0.6 dynamic_slice.22
  69.4 0.6 iota_add_fusion.5
  70.1 6.6 %fusion.68 = bf16[8,512,512]{2,1,0:T(8,128)(2,1)} fusion(bf16[8,512,512]{2,1,0:T(8,128)(2,1)} %get-tuple-element.278, s32[]{:T(128)} %get-tuple-element.277, bf16[2048,512]{1,0:T(8,128)(2,1)} %get-tuple-element.287, s32[2048]{0:T(1024)S(1)} %bitcast.126, s32[2048]{0:T(1024)S(1)} %bitcast.127, s32[2048]{0:T(1024)S(1)} %bitcast.128, ...), kind=kOutput, calls=%fused_computation.41.clone.1 | convolution fusion | flops 1105723392 | bytes 2705920 | tf_op jit(solution)/shard_map/while/body/eval_jaxpr/dot_general | solution.py:19
  76.7 0.2 all-reduce.6.cloned.1.call-start
  77.0 4.6 fusion.41
  81.5 39.8 %while.22 = (s32[]{:T(128)}, bf16[4,512,512]{2,1,0:T(8,128)(2,1)}, s32[2048,15]{0,1:T(8,128)S(1)}, s32[4]{0:T(128)S(1)}, bf16[2048,512]{1,0:T(8,128)(2,1)}, /*index=5*/s32[]{:T(128)}) while((s32[]{:T(128)}, bf16[4,512,512]{2,1,0:T(8,128)(2,1)}, s32[2048,15]{0,1:T(8,128)S(1)}, s32[4]{0:T(128)S(1)}, bf16[2048,512]{1,0:T(8,128)(2,1)}, ...), condition=%wide.region_1.2_spmd.clone, body=%wide.region_0.1_spmd.clone.sunk | while | flops 1121452544 | bytes 2994773 | solution.py:23
  81.5 0.1 fusion.64
  81.6 0.6 dynamic_slice.21
  82.2 0.6 iota_add_fusion.4
  82.9 8.6 %fusion.65 = bf16[4,512,512]{2,1,0:T(8,128)(2,1)} fusion(bf16[4,512,512]{2,1,0:T(8,128)(2,1)} %get-tuple-element.260, s32[]{:T(128)} %get-tuple-element.259, bf16[2048,512]{1,0:T(8,128)(2,1)} %get-tuple-element.269, s32[2048]{0:T(1024)S(1)} %bitcast.111, s32[2048]{0:T(1024)S(1)} %bitcast.112, s32[2048]{0:T(1024)S(1)} %bitcast.113, ...), kind=kOutput, calls=%fused_computation.23.clone.1 | convolution fusion | flops 1121452032 | bytes 2746880 | tf_op jit(solution)/shard_map/while/body/eval_jaxpr/dot_general | solution.py:19
  91.6 0.6 dynamic_slice.21
  92.2 0.6 iota_add_fusion.4
  92.9 8.6 %fusion.65 = bf16[4,512,512]{2,1,0:T(8,128)(2,1)} fusion(bf16[4,512,512]{2,1,0:T(8,128)(2,1)} %get-tuple-element.260, s32[]{:T(128)} %get-tuple-element.259, bf16[2048,512]{1,0:T(8,128)(2,1)} %get-tuple-element.269, s32[2048]{0:T(1024)S(1)} %bitcast.111, s32[2048]{0:T(1024)S(1)} %bitcast.112, s32[2048]{0:T(1024)S(1)} %bitcast.113, ...), kind=kOutput, calls=%fused_computation.23.clone.1 | convolution fusion | flops 1121452032 | bytes 2746880 | tf_op jit(solution)/shard_map/while/body/eval_jaxpr/dot_general | solution.py:19
  101.5 0.6 dynamic_slice.21
  102.2 0.6 iota_add_fusion.4
  102.8 8.6 %fusion.65 = bf16[4,512,512]{2,1,0:T(8,128)(2,1)} fusion(bf16[4,512,512]{2,1,0:T(8,128)(2,1)} %get-tuple-element.260, s32[]{:T(128)} %get-tuple-element.259, bf16[2048,512]{1,0:T(8,128)(2,1)} %get-tuple-element.269, s32[2048]{0:T(1024)S(1)} %bitcast.111, s32[2048]{0:T(1024)S(1)} %bitcast.112, s32[2048]{0:T(1024)S(1)} %bitcast.113, ...), kind=kOutput, calls=%fused_computation.23.clone.1 | convolution fusion | flops 1121452032 | bytes 2746880 | tf_op jit(solution)/shard_map/while/body/eval_jaxpr/dot_general | solution.py:19
  111.5 0.6 dynamic_slice.21
  112.1 0.6 iota_add_fusion.4
  112.8 8.6 %fusion.65 = bf16[4,512,512]{2,1,0:T(8,128)(2,1)} fusion(bf16[4,512,512]{2,1,0:T(8,128)(2,1)} %get-tuple-element.260, s32[]{:T(128)} %get-tuple-element.259, bf16[2048,512]{1,0:T(8,128)(2,1)} %get-tuple-element.269, s32[2048]{0:T(1024)S(1)} %bitcast.111, s32[2048]{0:T(1024)S(1)} %bitcast.112, s32[2048]{0:T(1024)S(1)} %bitcast.113, ...), kind=kOutput, calls=%fused_computation.23.clone.1 | convolution fusion | flops 1121452032 | bytes 2746880 | tf_op jit(solution)/shard_map/while/body/eval_jaxpr/dot_general | solution.py:19
  121.4 4.6 fusion.50
  126.0 66.5 %all-reduce.4.cloned.1.call-done = bf16[4096,512]{1,0:T(8,128)(2,1)} async-done(((bf16[4096,512]{1,0:T(8,128)(2,1)}), bf16[4096,512]{1,0:T(8,128)(2,1)}) %all-reduce.4.cloned.1.call-update) | async-done | bytes 4194320 | tf_op jit(solution)/shard_map/psum | solution.py:44
  192.5 3.6 add_bitcast_fusion
  196.0 266.8 %all-reduce.6.cloned.1.call-done = (f32[768,512]{0,1:T(8,128)}, f32[512,512]{1,0:T(8,128)}) async-done(((f32[768,512]{0,1:T(8,128)}, f32[512,512]{1,0:T(8,128)}), (f32[768,512]{0,1:T(8,128)}, f32[512,512]{1,0:T(8,128)})) %all-reduce.6.cloned.1.call-update) | async-done | bytes 2621456 | tf_op jit(solution)/shard_map/psum | solution.py:51
  462.9 3.0 copy.10
  465.9 2.3 copy.30
  (25 shorter events, 0.8 us)
Async XLA Ops:
  7.2 114.2 %copy-start = (bf16[2048,768]{1,0:T(8,128)(2,1)S(1)}, bf16[2048,768]{1,0:T(8,128)(2,1)}, u32[]{:S(2)}) copy-start(bf16[2048,768]{1,0:T(8,128)(2,1)} %param.19) | copy-start | bytes 9437188
  7.2 185.3 %all-reduce.4.cloned.1.call-start = ((), (), s32[]{:S(2)}) async-start(), calls=%async_computation | async-start | bytes 8388608 | tf_op jit(solution)/shard_map/psum | solution.py:44
  8.1 5.2 %copy-start.2 = (s32[2048,10]{0,1:T(8,128)S(1)}, s32[2048,10]{0,1:T(8,128)}, u32[]{:S(2)}) copy-start(s32[2048,10]{0,1:T(8,128)} %param.16) | copy-start | bytes 245764
  76.7 4.8 %copy-start.1 = (s32[2048,15]{0,1:T(8,128)S(1)}, s32[2048,15]{0,1:T(8,128)}, u32[]{:S(2)}) copy-start(s32[2048,15]{0,1:T(8,128)} %param.17) | copy-start | bytes 368644
  76.7 386.1 %all-reduce.6.cloned.1.call-start = ((), (), s32[]{:S(2)}) async-start(), calls=%async_computation.1 | async-start | bytes 5242880 | tf_op jit(solution)/shard_map/psum | solution.py:51
Sparse Core Ops, SparseCore 0:
  76.8 115.5 all-reduce.3
  198.6 264.2 all-reduce.5
where the time goes:
time: 476 us; the launch traced here: 475 us
  waiting for transfers between devices  333 us (70%)
  matrix products  105 us (22%)
  between operations  14.9 us (3%)
  local copies, waits for them, and re-layouts  13.6 us (3%)
  other arithmetic  7.56 us (2%)
    psum x1, waiting for transfers between devices, on_device(): total_one, total_two = lax.psum((grad_one, grad_two), ('clique', 'copy'))  267 us
    dot_general x12, matrix products, one_block(): jnp.dot(counts.astype(jnp.bfloat16), row_grad, preferred_element_type=jnp...  87.3 us
    psum x1, waiting for transfers between devices, on_device(): summed = lax.psum(hot_part, 'clique').astype(jnp.float32)  66.5 us
  transfers between devices with their start and end apart: 2, of which 2 were waited for; matrix products, arithmetic and copies ran while one was open for 10% of the time, Pallas kernels for 0%

commit v1 on v0

--- a/solution.py
+++ b/solution.py
@@ -48,7 +48,7 @@
     grad_one = grad_one + jnp.dot(
         hot_feats.T, owned.astype(jnp.bfloat16), preferred_element_type=jnp.float32
     )
-    total_one, total_two = lax.psum((grad_one, grad_two), ("clique", "copy"))
+    total_one, total_two = lax.psum(lax.psum((grad_one, grad_two), "copy"), "clique")
     return (total_one, total_two)
 
 

time: 476 us -> 548 us (1.15)
  waiting for transfers between devices: 333 us -> 403 us
    psum x1 -> x2, waiting for transfers between devices: 267 us -> 336 us  [the longest x1 234 us: on_device(): lax.psum((grad_one, grad_two), 'copy')]
  transfers between devices with their start and end apart: 2 -> 3, of which waited for: 2 -> 3; matrix products, arithmetic and copies ran while one was open for 10% -> 9% of each run, Pallas kernels for 0% -> 0%
where the time goes in v1:
time: 548 us; the launch traced here: 544 us
  waiting for transfers between devices  403 us (74%)
  matrix products  105 us (19%)
  between operations  14.6 us (3%)
  local copies, waits for them, and re-layouts  13.7 us (2%)
  other arithmetic  7.46 us (1%)
    psum x1, waiting for transfers between devices, on_device(): lax.psum((grad_one, grad_two), 'copy')  234 us
    psum x1, waiting for transfers between devices, on_device(): lax.psum(lax.psum((grad_one, grad_two), 'copy'), 'clique')  102 us
    dot_general x12, matrix products, one_block(): jnp.dot(counts.astype(jnp.bfloat16), row_grad, preferred_element_type=jnp...  87.3 us
    psum x1, waiting for transfers between devices, on_device(): summed = lax.psum(hot_part, 'clique').astype(jnp.float32)  66.6 us
  transfers between devices with their start and end apart: 3, of which 3 were waited for; matrix products, arithmetic and copies ran while one was open for 9% of the time, Pallas kernels for 0%

profile of v1, /device:TPU:2, one launch (start us, length us, event | category | flops | bytes accessed | tf_op | source)
XLA Modules:
  0.0 544.1 jit_solution(16237619258299428963)
XLA Ops:
  8.1 5.2 select_convert_fusion
  13.3 63.5 %while.23 = (s32[]{:T(128)}, bf16[8,512,512]{2,1,0:T(8,128)(2,1)}, s32[2048,10]{0,1:T(8,128)S(1)}, s32[8]{0:T(128)S(1)}, bf16[2048,512]{1,0:T(8,128)(2,1)}, /*index=5*/s32[]{:T(128)}) while((s32[]{:T(128)}, bf16[8,512,512]{2,1,0:T(8,128)(2,1)}, s32[2048,10]{0,1:T(8,128)S(1)}, s32[8]{0:T(128)S(1)}, bf16[2048,512]{1,0:T(8,128)(2,1)}, ...), condition=%wide.region_3.4_spmd.clone, body=%wide.region_2.3_spmd.clone.sunk | while | flops 1105723904 | bytes 2871893 | solution.py:23
  13.3 0.7 dynamic_slice.22
  14.0 0.6 iota_add_fusion.5
  14.6 6.6 %fusion.68 = bf16[8,512,512]{2,1,0:T(8,128)(2,1)} fusion(bf16[8,512,512]{2,1,0:T(8,128)(2,1)} %get-tuple-element.280, s32[]{:T(128)} %get-tuple-element.279, bf16[2048,512]{1,0:T(8,128)(2,1)} %get-tuple-element.289, s32[2048]{0:T(1024)S(1)} %bitcast.126, s32[2048]{0:T(1024)S(1)} %bitcast.127, s32[2048]{0:T(1024)S(1)} %bitcast.128, ...), kind=kOutput, calls=%fused_computation.41.clone.1 | convolution fusion | flops 1105723392 | bytes 2705920 | tf_op jit(solution)/shard_map/while/body/eval_jaxpr/dot_general | solution.py:19
  21.2 0.7 dynamic_slice.22
  21.9 0.6 iota_add_fusion.5
  22.5 6.6 %fusion.68 = bf16[8,512,512]{2,1,0:T(8,128)(2,1)} fusion(bf16[8,512,512]{2,1,0:T(8,128)(2,1)} %get-tuple-element.280, s32[]{:T(128)} %get-tuple-element.279, bf16[2048,512]{1,0:T(8,128)(2,1)} %get-tuple-element.289, s32[2048]{0:T(1024)S(1)} %bitcast.126, s32[2048]{0:T(1024)S(1)} %bitcast.127, s32[2048]{0:T(1024)S(1)} %bitcast.128, ...), kind=kOutput, calls=%fused_computation.41.clone.1 | convolution fusion | flops 1105723392 | bytes 2705920 | tf_op jit(solution)/shard_map/while/body/eval_jaxpr/dot_general | solution.py:19
  29.2 0.7 dynamic_slice.22
  29.8 0.6 iota_add_fusion.5
  30.5 6.6 %fusion.68 = bf16[8,512,512]{2,1,0:T(8,128)(2,1)} fusion(bf16[8,512,512]{2,1,0:T(8,128)(2,1)} %get-tuple-element.280, s32[]{:T(128)} %get-tuple-element.279, bf16[2048,512]{1,0:T(8,128)(2,1)} %get-tuple-element.289, s32[2048]{0:T(1024)S(1)} %bitcast.126, s32[2048]{0:T(1024)S(1)} %bitcast.127, s32[2048]{0:T(1024)S(1)} %bitcast.128, ...), kind=kOutput, calls=%fused_computation.41.clone.1 | convolution fusion | flops 1105723392 | bytes 2705920 | tf_op jit(solution)/shard_map/while/body/eval_jaxpr/dot_general | solution.py:19
  37.1 0.7 dynamic_slice.22
  37.8 0.6 iota_add_fusion.5
  38.4 6.6 %fusion.68 = bf16[8,512,512]{2,1,0:T(8,128)(2,1)} fusion(bf16[8,512,512]{2,1,0:T(8,128)(2,1)} %get-tuple-element.280, s32[]{:T(128)} %get-tuple-element.279, bf16[2048,512]{1,0:T(8,128)(2,1)} %get-tuple-element.289, s32[2048]{0:T(1024)S(1)} %bitcast.126, s32[2048]{0:T(1024)S(1)} %bitcast.127, s32[2048]{0:T(1024)S(1)} %bitcast.128, ...), kind=kOutput, calls=%fused_computation.41.clone.1 | convolution fusion | flops 1105723392 | bytes 2705920 | tf_op jit(solution)/shard_map/while/body/eval_jaxpr/dot_general | solution.py:19
  45.0 0.7 dynamic_slice.22
  45.7 0.6 iota_add_fusion.5
  46.3 6.6 %fusion.68 = bf16[8,512,512]{2,1,0:T(8,128)(2,1)} fusion(bf16[8,512,512]{2,1,0:T(8,128)(2,1)} %get-tuple-element.280, s32[]{:T(128)} %get-tuple-element.279, bf16[2048,512]{1,0:T(8,128)(2,1)} %get-tuple-element.289, s32[2048]{0:T(1024)S(1)} %bitcast.126, s32[2048]{0:T(1024)S(1)} %bitcast.127, s32[2048]{0:T(1024)S(1)} %bitcast.128, ...), kind=kOutput, calls=%fused_computation.41.clone.1 | convolution fusion | flops 1105723392 | bytes 2705920 | tf_op jit(solution)/shard_map/while/body/eval_jaxpr/dot_general | solution.py:19
  53.0 0.7 dynamic_slice.22
  53.6 0.6 iota_add_fusion.5
  54.3 6.6 %fusion.68 = bf16[8,512,512]{2,1,0:T(8,128)(2,1)} fusion(bf16[8,512,512]{2,1,0:T(8,128)(2,1)} %get-tuple-element.280, s32[]{:T(128)} %get-tuple-element.279, bf16[2048,512]{1,0:T(8,128)(2,1)} %get-tuple-element.289, s32[2048]{0:T(1024)S(1)} %bitcast.126, s32[2048]{0:T(1024)S(1)} %bitcast.127, s32[2048]{0:T(1024)S(1)} %bitcast.128, ...), kind=kOutput, calls=%fused_computation.41.clone.1 | convolution fusion | flops 1105723392 | bytes 2705920 | tf_op jit(solution)/shard_map/while/body/eval_jaxpr/dot_general | solution.py:19
  60.9 0.7 dynamic_slice.22
  61.6 0.6 iota_add_fusion.5
  62.2 6.6 %fusion.68 = bf16[8,512,512]{2,1,0:T(8,128)(2,1)} fusion(bf16[8,512,512]{2,1,0:T(8,128)(2,1)} %get-tuple-element.280, s32[]{:T(128)} %get-tuple-element.279, bf16[2048,512]{1,0:T(8,128)(2,1)} %get-tuple-element.289, s32[2048]{0:T(1024)S(1)} %bitcast.126, s32[2048]{0:T(1024)S(1)} %bitcast.127, s32[2048]{0:T(1024)S(1)} %bitcast.128, ...), kind=kOutput, calls=%fused_computation.41.clone.1 | convolution fusion | flops 1105723392 | bytes 2705920 | tf_op jit(solution)/shard_map/while/body/eval_jaxpr/dot_general | solution.py:19
  68.9 0.7 dynamic_slice.22
  69.5 0.6 iota_add_fusion.5
  70.1 6.6 %fusion.68 = bf16[8,512,512]{2,1,0:T(8,128)(2,1)} fusion(bf16[8,512,512]{2,1,0:T(8,128)(2,1)} %get-tuple-element.280, s32[]{:T(128)} %get-tuple-element.279, bf16[2048,512]{1,0:T(8,128)(2,1)} %get-tuple-element.289, s32[2048]{0:T(1024)S(1)} %bitcast.126, s32[2048]{0:T(1024)S(1)} %bitcast.127, s32[2048]{0:T(1024)S(1)} %bitcast.128, ...), kind=kOutput, calls=%fused_computation.41.clone.1 | convolution fusion | flops 1105723392 | bytes 2705920 | tf_op jit(solution)/shard_map/while/body/eval_jaxpr/dot_general | solution.py:19
  76.8 0.2 all-reduce.8.cloned.1.call-start
  77.1 4.5 fusion.41
  81.6 39.7 %while.22 = (s32[]{:T(128)}, bf16[4,512,512]{2,1,0:T(8,128)(2,1)}, s32[2048,15]{0,1:T(8,128)S(1)}, s32[4]{0:T(128)S(1)}, bf16[2048,512]{1,0:T(8,128)(2,1)}, /*index=5*/s32[]{:T(128)}) while((s32[]{:T(128)}, bf16[4,512,512]{2,1,0:T(8,128)(2,1)}, s32[2048,15]{0,1:T(8,128)S(1)}, s32[4]{0:T(128)S(1)}, bf16[2048,512]{1,0:T(8,128)(2,1)}, ...), condition=%wide.region_1.2_spmd.clone, body=%wide.region_0.1_spmd.clone.sunk | while | flops 1121452544 | bytes 2994773 | solution.py:23
  81.7 0.6 dynamic_slice.21
  82.3 0.6 iota_add_fusion.4
  82.9 8.6 %fusion.65 = bf16[4,512,512]{2,1,0:T(8,128)(2,1)} fusion(bf16[4,512,512]{2,1,0:T(8,128)(2,1)} %get-tuple-element.262, s32[]{:T(128)} %get-tuple-element.261, bf16[2048,512]{1,0:T(8,128)(2,1)} %get-tuple-element.271, s32[2048]{0:T(1024)S(1)} %bitcast.111, s32[2048]{0:T(1024)S(1)} %bitcast.112, s32[2048]{0:T(1024)S(1)} %bitcast.113, ...), kind=kOutput, calls=%fused_computation.23.clone.1 | convolution fusion | flops 1121452032 | bytes 2746880 | tf_op jit(solution)/shard_map/while/body/eval_jaxpr/dot_general | solution.py:19
  91.6 0.6 dynamic_slice.21
  92.2 0.6 iota_add_fusion.4
  92.8 8.6 %fusion.65 = bf16[4,512,512]{2,1,0:T(8,128)(2,1)} fusion(bf16[4,512,512]{2,1,0:T(8,128)(2,1)} %get-tuple-element.262, s32[]{:T(128)} %get-tuple-element.261, bf16[2048,512]{1,0:T(8,128)(2,1)} %get-tuple-element.271, s32[2048]{0:T(1024)S(1)} %bitcast.111, s32[2048]{0:T(1024)S(1)} %bitcast.112, s32[2048]{0:T(1024)S(1)} %bitcast.113, ...), kind=kOutput, calls=%fused_computation.23.clone.1 | convolution fusion | flops 1121452032 | bytes 2746880 | tf_op jit(solution)/shard_map/while/body/eval_jaxpr/dot_general | solution.py:19
  101.5 0.6 dynamic_slice.21
  102.1 0.6 iota_add_fusion.4
  102.8 8.6 %fusion.65 = bf16[4,512,512]{2,1,0:T(8,128)(2,1)} fusion(bf16[4,512,512]{2,1,0:T(8,128)(2,1)} %get-tuple-element.262, s32[]{:T(128)} %get-tuple-element.261, bf16[2048,512]{1,0:T(8,128)(2,1)} %get-tuple-element.271, s32[2048]{0:T(1024)S(1)} %bitcast.111, s32[2048]{0:T(1024)S(1)} %bitcast.112, s32[2048]{0:T(1024)S(1)} %bitcast.113, ...), kind=kOutput, calls=%fused_computation.23.clone.1 | convolution fusion | flops 1121452032 | bytes 2746880 | tf_op jit(solution)/shard_map/while/body/eval_jaxpr/dot_general | solution.py:19
  111.5 0.6 dynamic_slice.21
  112.1 0.6 iota_add_fusion.4
  112.7 8.6 %fusion.65 = bf16[4,512,512]{2,1,0:T(8,128)(2,1)} fusion(bf16[4,512,512]{2,1,0:T(8,128)(2,1)} %get-tuple-element.262, s32[]{:T(128)} %get-tuple-element.261, bf16[2048,512]{1,0:T(8,128)(2,1)} %get-tuple-element.271, s32[2048]{0:T(1024)S(1)} %bitcast.111, s32[2048]{0:T(1024)S(1)} %bitcast.112, s32[2048]{0:T(1024)S(1)} %bitcast.113, ...), kind=kOutput, calls=%fused_computation.23.clone.1 | convolution fusion | flops 1121452032 | bytes 2746880 | tf_op jit(solution)/shard_map/while/body/eval_jaxpr/dot_general | solution.py:19
  121.3 4.6 fusion.50
  125.9 66.6 %all-reduce.6.cloned.1.call-done = bf16[4096,512]{1,0:T(8,128)(2,1)} async-done(((bf16[4096,512]{1,0:T(8,128)(2,1)}), bf16[4096,512]{1,0:T(8,128)(2,1)}) %all-reduce.6.cloned.1.call-update) | async-done | bytes 4194320 | tf_op jit(solution)/shard_map/psum | solution.py:44
  192.6 3.6 add_bitcast_fusion
  196.2 234.1 %all-reduce.8.cloned.1.call-done = (f32[768,512]{0,1:T(8,128)}, f32[512,512]{1,0:T(8,128)}) async-done(((f32[768,512]{0,1:T(8,128)}, f32[512,512]{1,0:T(8,128)}), (f32[768,512]{0,1:T(8,128)}, f32[512,512]{1,0:T(8,128)})) %all-reduce.8.cloned.1.call-update) | async-done | bytes 2621456 | tf_op jit(solution)/shard_map/psum | solution.py:51
  430.3 102.0 %all-reduce.10.cloned.1.call-done = (f32[768,512]{0,1:T(8,128)}, f32[512,512]{1,0:T(8,128)}) async-done(((f32[768,512]{0,1:T(8,128)}, f32[512,512]{1,0:T(8,128)}), (f32[768,512]{0,1:T(8,128)}, f32[512,512]{1,0:T(8,128)})) %all-reduce.10.cloned.1.call-update) | async-done | bytes 2621456 | tf_op jit(solution)/shard_map/psum | solution.py:51
  532.3 3.0 copy.10
  535.4 2.3 copy.32
  (28 shorter events, 0.9 us)
Async XLA Ops:
  7.2 114.2 %copy-start = (bf16[2048,768]{1,0:T(8,128)(2,1)S(1)}, bf16[2048,768]{1,0:T(8,128)(2,1)}, u32[]{:S(2)}) copy-start(bf16[2048,768]{1,0:T(8,128)(2,1)} %param.19) | copy-start | bytes 9437188
  7.2 185.4 %all-reduce.6.cloned.1.call-start = ((), (), s32[]{:S(2)}) async-start(), calls=%async_computation | async-start | bytes 8388608 | tf_op jit(solution)/shard_map/psum | solution.py:44
  8.1 5.2 copy-start.2
  76.8 4.8 copy-start.1
  76.8 353.5 %all-reduce.8.cloned.1.call-start = ((), (), s32[]{:S(2)}) async-start(), calls=%async_computation.1 | async-start | bytes 5242880 | tf_op jit(solution)/shard_map/psum | solution.py:51
  196.2 336.2 %all-reduce.10.cloned.1.call-start = ((), (), s32[]{:S(2)}) async-start(), calls=%async_computation.2 | async-start | bytes 5242880 | tf_op jit(solution)/shard_map/psum | solution.py:51
Sparse Core Ops, SparseCore 0:
  76.9 115.6 all-reduce.5
  196.3 233.9 all-reduce.7
  433.0 99.2 all-reduce.9
